TPU v7x, 32 devices: a whole 2x2x4 slice. The times are simulated.
32 devices in a mesh: py: 4 (over y, x), pz: 8 (over z, core).
Axes of the slice: x: 2, y: 2, z: 4, core: 2. Of those that a mesh axis runs over, the one named last changes fastest.
Arguments:
- field_one: float32 [256, 256, 512], P('py', 'pz'), may hold values from -6 to 6
- field_two: float32 [256, 256, 512], P('py', 'pz'), may hold values from -6 to 6
- coef: float32 [2, 2, 8], replicated, may hold values from -4 to 4
Outputs:
- potential_one: float32 [256, 256, 512], P('py', 'pz')
- potential_two: float32 [256, 256, 512], P('py', 'pz')
All inputs are finite; a program needn't handle non-finite values.
Results may differ from a plain program's by a relative error of at most 0.00013.
Values sent between devices are 32-bit elements; how exact they have to be, the bound alone decides.
No kernel may reach another device: no remote copies, remote signals or barrier semaphores. Data moves between devices by JAX's collectives and lax.ppermute only.
A program may use at most 256 MiB of HBM per device.

v0:
```python
import math
import jax
import jax.numpy as jnp
from jax import lax
from jax.sharding import PartitionSpec as P

HIGH = lax.Precision.HIGHEST


def padded_2(value, sides, width):
    for axis, dim in sides:
        size, length = (lax.axis_size(axis), value.shape[dim])
        up = [(i, (i + 1) % size) for i in range(size)]
        down = [(j, i) for i, j in up]
        last = lax.slice_in_dim(value, length - width, length, axis=dim)
        leading = lax.slice_in_dim(value, 0, width, axis=dim)
        before = lax.ppermute(last, axis, up)
        after = lax.ppermute(leading, axis, down)
        value = jnp.concatenate([before, value, after], axis=dim)
    return value


def freq_at(position, length):
    paired = position // 2
    odd_bit = position % 2
    inner = jnp.where(odd_bit == 0, paired, length - paired)
    return jnp.where(paired == 0, odd_bit * (length // 2), inner)


def scaled_signed(freq, length):
    return jnp.where(freq > length // 2, freq - length, freq).astype(jnp.float32) / length


def forward_table(length):
    indices = jnp.arange(length, dtype=jnp.int32)
    freq = freq_at(indices, length)
    phase = indices[:, None] * freq[None, :] % length
    angle = 2.0 * math.pi / length * phase.astype(jnp.float32)
    return (jnp.cos(angle), jnp.sin(angle))


def inverse_table(length):
    cosine, sine = forward_table(length)
    return (cosine.T / length, sine.T / length)


def contract(form, data, table):
    return jnp.einsum(form, data, table, precision=HIGH)


def complex_apply(form, real_part, imag_part, cosine, sine, sign):
    if imag_part is None:
        return (contract(form, real_part, cosine), -sign * contract(form, real_part, sine))
    real_out = contract(form, real_part, cosine) + sign * contract(form, imag_part, sine)
    imag_out = contract(form, imag_part, cosine) - sign * contract(form, real_part, sine)
    return (real_out, imag_out)


def make_kernel(coef, freqs, lengths):
    radius = scaled_signed(freqs[0], lengths[0]) ** 2 + scaled_signed(freqs[1], lengths[1]) ** 2
    radius = radius + scaled_signed(freqs[2], lengths[2]) ** 2
    ratio = 4.0 * radius / 3.0
    volume = ratio * jnp.sqrt(ratio)
    basis_count = coef.shape[2]
    centres = (jnp.arange(basis_count, dtype=jnp.float32) + 0.5) / basis_count
    basis = jnp.exp(-jnp.square((volume[None] - centres[:, None, None, None]) * basis_count))
    kernel = jnp.einsum("abr,rkxm->abkxm", coef, basis, precision=HIGH)
    return kernel


def shards(field_one, field_two, coef):
    y_local, z_local, x_count = field_one.shape
    py_count = lax.axis_size("py")
    pz_count = lax.axis_size("pz")
    y_count = y_local * py_count
    z_count = z_local * pz_count
    x_block = x_count // py_count
    ky_block = y_count // pz_count
    cells = y_local * z_local
    fields = jnp.stack([field_one, field_two])
    along_x = (4.0 * fields + jnp.roll(fields, 1, 3) + jnp.roll(fields, -1, 3)) / 6.0
    padded = padded_2(along_x, (("py", 1), ("pz", 2)), 1)
    along_y = (4.0 * padded[:, 1:-1] + padded[:, 2:] + padded[:, :-2]) / 6.0
    smoothed = (4.0 * along_y[:, :, 1:-1] + along_y[:, :, 2:] + along_y[:, :, :-2]) / 6.0
    flat = smoothed.reshape(2, cells, x_count)
    x_cos, x_sin = forward_table(x_count)
    real_part, imag_part = complex_apply("bsx,xq->bqs", flat, None, x_cos, x_sin, 1.0)
    batch = real_part.shape[0]
    y_cos, y_sin = forward_table(y_count)
    z_cos, z_sin = forward_table(z_count)
    zi_cos, zi_sin = inverse_table(z_count)
    yi_cos, yi_sin = inverse_table(y_count)
    xi_cos, xi_sin = inverse_table(x_count)
    real_in = lax.all_to_all(real_part, "py", split_axis=1, concat_axis=2, tiled=True)
    imag_in = lax.all_to_all(imag_part, "py", split_axis=1, concat_axis=2, tiled=True)
    items = real_in.shape[0]

    def relay(values):
        values = values.reshape(items, x_block, y_count, z_local).transpose(0, 2, 1, 3)
        return values.reshape(items, y_count, x_block * z_local)

    real_part, imag_part = complex_apply(
        "byc,yk->bkc", relay(real_in), relay(imag_in), y_cos, y_sin, 1.0
    )
    real_in = lax.all_to_all(real_part, "pz", split_axis=1, concat_axis=2, tiled=True)
    imag_in = lax.all_to_all(imag_part, "pz", split_axis=1, concat_axis=2, tiled=True)
    lines_items = real_in.shape[0]

    def relay(values):
        values = values.reshape(lines_items, ky_block, pz_count, x_block, z_local).transpose(
            0, 1, 3, 2, 4
        )
        return values.reshape(lines_items, ky_block, x_block, z_count)

    real_part, imag_part = complex_apply(
        "bkxz,zm->bkxm", relay(real_in), relay(imag_in), z_cos, z_sin, 1.0
    )
    ky_start = lax.axis_index("pz") * ky_block
    kx_start = lax.axis_index("py") * x_block
    freq_y = freq_at(ky_start + jnp.arange(ky_block, dtype=jnp.int32), y_count)
    freq_x = freq_at(kx_start + jnp.arange(x_block, dtype=jnp.int32), x_count)
    freq_z = freq_at(jnp.arange(z_count, dtype=jnp.int32), z_count)
    kernel = make_kernel(
        coef,
        (freq_y[:, None, None], freq_x[None, :, None], freq_z[None, None, :]),
        (y_count, x_count, z_count),
    )
    real_next = kernel[:, 0] * real_part[0] + kernel[:, 1] * real_part[1]
    imag_next = kernel[:, 0] * imag_part[0] + kernel[:, 1] * imag_part[1]
    real_part = real_next
    imag_part = imag_next
    real_part, imag_part = complex_apply(
        "bkxm,mz->bkxz", real_part, imag_part, zi_cos, zi_sin, -1.0
    )

    def relay_back(values):
        values = values.reshape(batch, ky_block, x_block, pz_count, z_local).transpose(
            0, 1, 3, 2, 4
        )
        return values.reshape(batch, ky_block, pz_count * x_block * z_local)

    real_part = relay_back(real_part)
    imag_part = relay_back(imag_part)
    real_in = lax.all_to_all(real_part, "pz", split_axis=2, concat_axis=1, tiled=True)
    imag_in = lax.all_to_all(imag_part, "pz", split_axis=2, concat_axis=1, tiled=True)
    back_items = real_in.shape[0]
    real_out, imag_out = complex_apply("bkc,ky->byc", real_in, imag_in, yi_cos, yi_sin, -1.0)

    def relay(values):
        values = values.reshape(back_items, y_count, x_block, z_local).transpose(0, 2, 1, 3)
        return values.reshape(back_items, x_block, y_count * z_local)

    real_part = relay(real_out)
    imag_part = relay(imag_out)
    real_in = lax.all_to_all(real_part, "py", split_axis=2, concat_axis=1, tiled=True)
    imag_in = lax.all_to_all(imag_part, "py", split_axis=2, concat_axis=1, tiled=True)
    result = contract("bqs,qx->bsx", real_in, xi_cos) - contract("bqs,qx->bsx", imag_in, xi_sin)
    return (
        result[0].reshape(y_local, z_local, x_count),
        result[1].reshape(y_local, z_local, x_count),
    )


def solution(mesh):
    in_specs = (P("py", "pz", None), P("py", "pz", None), P())
    out_specs = (P("py", "pz", None), P("py", "pz", None))
    return jax.shard_map(shards, mesh=mesh, in_specs=in_specs, out_specs=out_specs, check_vma=False)
```

profile of v0, /device:TPU:0, one launch (start us, length us, event | category | flops | bytes accessed | tf_op | source)
XLA Modules:
  0.0 1785.4 jit_solution(6525902035825200465)
XLA Ops:
  56.9 36.3 %convolution_bitcast_fusion = f32[2,512,2048]{2,1,0:T(8,128)S(1)} fusion(f32[2,2048,512]{2,1,0:T(8,128)} %bitcast.222, s32[512]{0:T(512)S(1)} %fusion.138), kind=kOutput, calls=%fused_computation.64 | convolution fusion | flops 12888571904 | bytes 16779264 | tf_op jit(solution)/shard_map/bsx,xq->bqs/dot_general | solution.py:48
  110.0 48.6 %multiply_bitcast_fusion = f32[2,512,2048]{2,1,0:T(8,128)S(1)} fusion(f32[2,2048,512]{2,1,0:T(8,128)} %bitcast.223, s32[512]{0:T(512)S(1)} %fusion.138), kind=kOutput, calls=%fused_computation.54 | convolution fusion | flops 12890669056 | bytes 16779264 | tf_op jit(solution)/shard_map/bsx,xq->bqs/dot_general | solution.py:48
  169.8 33.0 %all-to-all-done = f32[2,512,2048]{2,0,1:T(2,128)} async-done(((f32[2,512,2048]{2,0,1:T(2,128)}), f32[2,512,2048]{2,0,1:T(2,128)}, u32[]{:S(2)}, u32[]{:S(2)}) %all-to-all-start) | async-done | bytes 8388640 | tf_op jit(solution)/shard_map/all_to_all | solution.py:94
  239.1 62.9 %all-to-all-done.1 = f32[2,512,2048]{2,0,1:T(2,128)} async-done(((f32[2,512,2048]{2,0,1:T(2,128)}), f32[2,512,2048]{2,0,1:T(2,128)}, u32[]{:S(2)}, u32[]{:S(2)}) %all-to-all-start.1) | async-done | bytes 8388640 | tf_op jit(solution)/shard_map/all_to_all | solution.py:95
  406.5 150.7 %all-to-all-done.2 = f32[2,256,4096]{2,0,1:T(2,128)} async-done(((f32[2,256,4096]{2,0,1:T(2,128)}), f32[2,256,4096]{2,0,1:T(2,128)}, u32[]{:S(2)}, u32[]{:S(2)}) %all-to-all-start.2) | async-done | bytes 8388640 | tf_op jit(solution)/shard_map/all_to_all | solution.py:105
  564.1 58.6 %fusion.10 = f32[2,2,32,128,256]{4,1,0,3,2:T(2,128)} fusion(f32[8]{0:T(128)S(1)} %add_multiply_fusion, f32[32,128,256]{2,1,0:T(8,128)S(1)} %sqrt_multiply_fusion, f32[2,2,8]{2,1,0:T(2,128)S(1)} %copy-done), kind=kOutput, calls=%fused_computation.19 | convolution fusion | flops 436207616 | bytes 20971680 | tf_op jit(solution)/shard_map/abr,rkxm->abkxm/dot_general | solution.py:67
  674.5 21.7 %copy.133 = f32[2,32,128,8,32]{2,4,3,1,0:T(8,128)} copy(f32[2,32,128,8,32]{4,2,3,1,0:T(8,128)} %bitcast.202) | data formatting | bytes 16777216 | tf_op jit(solution)/shard_map/transpose | solution.py:110
  715.9 30.5 %all-to-all-done.3 = f32[2,256,4096]{2,0,1:T(2,128)} async-done(((f32[2,256,4096]{2,0,1:T(2,128)}), f32[2,256,4096]{2,0,1:T(2,128)}, u32[]{:S(2)}, u32[]{:S(2)}) %all-to-all-start.3) | async-done | bytes 8388640 | tf_op jit(solution)/shard_map/all_to_all | solution.py:106
  778.0 21.7 %copy.140 = f32[2,32,128,8,32]{2,4,3,1,0:T(8,128)} copy(f32[2,32,128,8,32]{4,2,3,1,0:T(8,128)} %bitcast.203) | data formatting | bytes 16777216 | tf_op jit(solution)/shard_map/transpose | solution.py:110
  866.1 30.2 %fusion.27 = (f32[2,32,128,256]{3,0,2,1:T(2,128)}, f32[2,32,128,256]{3,0,2,1:T(2,128)}) fusion(f32[2,1,32,128,256]{4,1,0,3,2:T(1,128)} %get-tuple-element.5, f32[2,1,32,128,256]{4,1,0,3,2:T(1,128)} %get-tuple-element.4, f32[32,128,256]{2,1,0:T(8,128)} %get-tuple-element.20, f32[32,128,256]{2,1,0:T(8,128)} %get-tuple-element.21, ...), kind=kLoop, calls=%fused_computation.44 | loop fusion | flops 12582912 | bytes 50331648 | tf_op jit(solution)/shard_map/add | solution.py:128
  929.7 28.6 %copy.203 = f32[2,32,8,128,32]{1,0,4,3,2:T(2,128)} copy(f32[2,32,8,128,32]{3,4,2,1,0:T(8,128)} %bitcast.233) | data formatting | bytes 16777216 | tf_op jit(solution)/shard_map/reshape | solution.py:140
  958.3 35.4 %reshape.323 = f32[8,1,262144]{2,1,0:T(1,128)} reshape(f32[32768,2,32]{2,1,0:T(2,128)} %bitcast.204) | data formatting | bytes 16777216
  1034.7 28.6 %copy.208 = f32[2,32,8,128,32]{1,0,4,3,2:T(2,128)} copy(f32[2,32,8,128,32]{3,4,2,1,0:T(8,128)} %bitcast.234) | data formatting | bytes 16777216 | tf_op jit(solution)/shard_map/reshape | solution.py:140
  1063.4 35.8 %reshape.321 = f32[8,1,262144]{2,1,0:T(1,128)} reshape(f32[32768,2,32]{2,1,0:T(2,128)} %bitcast.205) | data formatting | bytes 16777216
  1099.2 83.5 %all-to-all-done.4 = f32[8,1,262144]{2,1,0:T(1,128)} async-done(((f32[8,1,262144]{2,1,0:T(1,128)}), f32[8,1,262144]{2,1,0:T(1,128)}, u32[]{:S(2)}, u32[]{:S(2)}) %all-to-all-start.4) | async-done | bytes 8388640 | tf_op jit(solution)/shard_map/all_to_all | solution.py:144
  1188.2 28.2 %reduce.1 = f32[8,262144]{1,0:T(8,128)} reduce(f32[8,1,262144]{2,1,0:T(1,128)} %all-to-all-done.4, f32[]{:T(128)} %broadcast.767), dimensions={1}, to_apply=%all_to_all.108.reduce_sub_computation | reduce | bytes 16777220 | tf_op jit(solution)/shard_map/all_to_all | solution.py:144
  1216.4 55.1 %reshape.324 = f32[32768,2,32]{2,1,0:T(2,128)} reshape(f32[8,262144]{1,0:T(8,128)} %reduce.1) | data formatting | bytes 16777216
  1271.4 40.0 %copy.205 = f32[2,32,8,4096]{3,1,2,0:T(8,128)} copy(f32[2,32,8,4096]{1,0,3,2:T(2,128)} %bitcast.206) | data formatting | bytes 16777216 | tf_op jit(solution)/shard_map/all_to_all | solution.py:144
  1311.4 60.1 %all-to-all-done.5 = f32[8,1,262144]{2,1,0:T(1,128)} async-done(((f32[8,1,262144]{2,1,0:T(1,128)}), f32[8,1,262144]{2,1,0:T(1,128)}, u32[]{:S(2)}, u32[]{:S(2)}) %all-to-all-start.5) | async-done | bytes 8388640 | tf_op jit(solution)/shard_map/all_to_all | solution.py:145
  1371.5 28.2 %reduce = f32[8,262144]{1,0:T(8,128)} reduce(f32[8,1,262144]{2,1,0:T(1,128)} %all-to-all-done.5, f32[]{:T(128)} %broadcast.767), dimensions={1}, to_apply=%all_to_all.112.reduce_sub_computation | reduce | bytes 16777220 | tf_op jit(solution)/shard_map/all_to_all | solution.py:145
  1399.7 54.9 %reshape.322 = f32[32768,2,32]{2,1,0:T(2,128)} reshape(f32[8,262144]{1,0:T(8,128)} %reduce) | data formatting | bytes 16777216
  1454.6 40.0 %copy.210 = f32[2,32,8,4096]{3,1,2,0:T(8,128)} copy(f32[2,32,8,4096]{1,0,3,2:T(2,128)} %bitcast.207) | data formatting | bytes 16777216 | tf_op jit(solution)/shard_map/all_to_all | solution.py:145
  1623.6 30.8 %all-to-all-done.7 = f32[2,128,8192]{1,0,2:T(2,128)} async-done(((f32[2,128,8192]{1,0,2:T(2,128)}), f32[2,128,8192]{1,0,2:T(2,128)}, u32[]{:S(2)}, u32[]{:S(2)}) %all-to-all-start.7) | async-done | bytes 8388640 | tf_op jit(solution)/shard_map/all_to_all | solution.py:156
  1684.1 67.9 %all-to-all-done.6 = f32[2,128,8192]{1,0,2:T(2,128)} async-done(((f32[2,128,8192]{1,0,2:T(2,128)}), f32[2,128,8192]{1,0,2:T(2,128)}, u32[]{:S(2)}, u32[]{:S(2)}) %all-to-all-start.6) | async-done | bytes 8388640 | tf_op jit(solution)/shard_map/all_to_all | solution.py:155
  (105 shorter events, 672.7 us)
Async XLA Ops:
  0.6 563.5 %copy-start = (f32[2,2,8]{2,1,0:T(2,128)S(1)}, f32[2,2,8]{2,1,0:T(2,128)}, u32[]{:S(2)}) copy-start(f32[2,2,8]{2,1,0:T(2,128)} %param.5) | copy-start | bytes 388
  0.6 13.7 copy-start.5
  0.7 13.6 copy-start.6
  25.9 8.3 collective-permute-start
  29.0 7.5 collective-permute-start.1
  37.0 8.5 collective-permute-start.2
  37.1 8.5 collective-permute-start.3
  40.6 69.3 %copy-start.9 = (s32[512]{0:T(512)}, s32[512]{0:T(512)S(1)}, u32[]{:S(2)}) copy-start(s32[512]{0:T(512)S(1)} %fusion.138) | copy-start | bytes 6148
  104.3 98.5 %all-to-all-start = ((f32[2,512,2048]{2,0,1:T(2,128)}), f32[2,512,2048]{2,0,1:T(2,128)}, u32[]{:S(2)}, u32[]{:S(2)}) async-start(f32[2,512,2048]{2,0,1:T(2,128)} %copy.120), calls=%async_computation | async-start | bytes 16777216 | tf_op jit(solution)/shard_map/all_to_all | solution.py:94
  202.8 99.2 %all-to-all-start.1 = ((f32[2,512,2048]{2,0,1:T(2,128)}), f32[2,512,2048]{2,0,1:T(2,128)}, u32[]{:S(2)}, u32[]{:S(2)}) async-start(f32[2,512,2048]{2,0,1:T(2,128)} %copy.126), calls=%async_computation.1 | async-start | bytes 16777216 | tf_op jit(solution)/shard_map/all_to_all | solution.py:95
  332.7 13.9 copy-start.3
  368.1 189.0 %all-to-all-start.2 = ((f32[2,256,4096]{2,0,1:T(2,128)}), f32[2,256,4096]{2,0,1:T(2,128)}, u32[]{:S(2)}, u32[]{:S(2)}) async-start(f32[2,256,4096]{2,0,1:T(2,128)} %copy.131), calls=%async_computation.2 | async-start | bytes 16777216 | tf_op jit(solution)/shard_map/all_to_all | solution.py:105
  557.1 189.2 %all-to-all-start.3 = ((f32[2,256,4096]{2,0,1:T(2,128)}), f32[2,256,4096]{2,0,1:T(2,128)}, u32[]{:S(2)}, u32[]{:S(2)}) async-start(f32[2,256,4096]{2,0,1:T(2,128)} %copy.138), calls=%async_computation.3 | async-start | bytes 16777216 | tf_op jit(solution)/shard_map/all_to_all | solution.py:106
  799.7 19.4 %copy-start.2 = (f32[2,32,128,8,32]{2,4,3,1,0:T(8,128)S(1)}, f32[2,32,128,8,32]{2,4,3,1,0:T(8,128)}, u32[]{:S(2)}) copy-start(f32[2,32,128,8,32]{2,4,3,1,0:T(8,128)} %copy.140) | copy-start | bytes 25165828
  799.7 40.6 %slice-start = ((s8[8388608]{0:T(1024)(128)(4,1)}), s8[4194304]{0:T(1024)(128)(4,1)S(1)}, s32[]{:S(2)}) async-start(s8[8388608]{0:T(1024)(128)(4,1)} %bitcast.213), calls=%async_computation.8 | async-start | bytes 8388608
  819.1 21.2 %slice-start.1 = ((s8[8388608]{0:T(1024)(128)(4,1)}), s8[4194304]{0:T(1024)(128)(4,1)S(1)}, s32[]{:S(2)}) async-start(s8[8388608]{0:T(1024)(128)(4,1)} %bitcast.213), calls=%async_computation.9 | async-start | bytes 8388608
  840.3 18.4 %copy-start.8 = (f32[2,32,128,256]{3,2,1,0:T(8,128)S(1)}, f32[2,32,128,256]{3,2,1,0:T(8,128)}, u32[]{:S(2)}) copy-start(f32[2,32,128,256]{3,2,1,0:T(8,128)} %convolution_add_fusion) | copy-start | bytes 25165828
  896.4 13.0 copy-start.4
  993.7 189.0 %all-to-all-start.4 = ((f32[8,1,262144]{2,1,0:T(1,128)}), f32[8,1,262144]{2,1,0:T(1,128)}, u32[]{:S(2)}, u32[]{:S(2)}) async-start(f32[8,1,262144]{2,1,0:T(1,128)} %reshape.323), calls=%async_computation.4 | async-start | bytes 16777216 | tf_op jit(solution)/shard_map/all_to_all | solution.py:144
  1182.7 188.8 %all-to-all-start.5 = ((f32[8,1,262144]{2,1,0:T(1,128)}), f32[8,1,262144]{2,1,0:T(1,128)}, u32[]{:S(2)}, u32[]{:S(2)}) async-start(f32[8,1,262144]{2,1,0:T(1,128)} %reshape.321), calls=%async_computation.5 | async-start | bytes 16777216 | tf_op jit(solution)/shard_map/all_to_all | solution.py:145
  1556.3 98.2 %all-to-all-start.7 = ((f32[2,128,8192]{1,0,2:T(2,128)}), f32[2,128,8192]{1,0,2:T(2,128)}, u32[]{:S(2)}, u32[]{:S(2)}) async-start(f32[2,128,8192]{1,0,2:T(2,128)} %copy.172), calls=%async_computation.7 | async-start | bytes 16777216 | tf_op jit(solution)/shard_map/all_to_all | solution.py:156
  1654.4 97.6 %all-to-all-start.6 = ((f32[2,128,8192]{1,0,2:T(2,128)}), f32[2,128,8192]{1,0,2:T(2,128)}, u32[]{:S(2)}, u32[]{:S(2)}) async-start(f32[2,128,8192]{1,0,2:T(2,128)} %copy.167), calls=%async_computation.6 | async-start | bytes 16777216 | tf_op jit(solution)/shard_map/all_to_all | solution.py:155
  1752.0 7.7 copy-start.7
  1759.7 25.5 %copy-start.1 = (f32[2,2,8]{2,1,0:T(2,128)S(1)}, f32[2,2,8]{2,1,0:T(2,128)}, u32[]{:S(2)}) copy-start(f32[2,2,8]{2,1,0:T(2,128)} %param.5) | copy-start | bytes 388
  (1 other events, 3.9 us)
where the time goes:
time: 1800 us; the launch traced here: 1790 us
  local copies, waits for them, and re-layouts  661 us (37%)
  waiting for transfers between devices  531 us (30%)
  matrix products  416 us (23%)
  other arithmetic  125 us (7%)
  starting transfers between devices  51 us (3%)
    dot_general x20, matrix products, contract(): return jnp.einsum(form, data, table, precision=HIGH)  357 us
    unnamed x30, local copies, waits for them, and re-layouts  181 us
    all_to_all x1, waiting for transfers between devices, shards(): lax.all_to_all(real_part, 'pz', split_axis=1, concat_axis=2, tiled=True)  151 us
    all_to_all x1, waiting for transfers between devices, shards(): lax.all_to_all(real_part, 'pz', split_axis=2, concat_axis=1, tiled=True)  83.5 us
    all_to_all x1, waiting for transfers between devices, shards(): lax.all_to_all(real_part, 'py', split_axis=2, concat_axis=1, tiled=True)  67.9 us
    all_to_all x1, waiting for transfers between devices, shards(): lax.all_to_all(imag_part, 'py', split_axis=1, concat_axis=2, tiled=True)  62.9 us
    all_to_all x1, waiting for transfers between devices, shards(): lax.all_to_all(imag_part, 'pz', split_axis=2, concat_axis=1, tiled=True)  60.1 us
    dot_general x1, matrix products, make_kernel(): kernel = jnp.einsum('abr,rkxm->abkxm', coef, basis, precision=HIGH)  58.6 us
  transfers between devices with their start and end apart: 12, of which 11 were waited for; matrix products, arithmetic and copies ran while one was open for 33% of the time, Pallas kernels for 0%

commit v1 on v0

--- a/solution.py
+++ b/solution.py
@@ -142,7 +142,10 @@
     real_part = relay_back(real_part)
     imag_part = relay_back(imag_part)
     real_in = lax.all_to_all(real_part, "pz", split_axis=2, concat_axis=1, tiled=True)
-    imag_in = lax.all_to_all(imag_part, "pz", split_axis=2, concat_axis=1, tiled=True)
+    imag_in = jnp.concatenate(
+        lax.all_to_all(jnp.stack(jnp.split(imag_part, lax.axis_size("pz"), axis=2)), "pz", 0, 0),
+        axis=1,
+    )
     back_items = real_in.shape[0]
     real_out, imag_out = complex_apply("bkc,ky->byc", real_in, imag_in, yi_cos, yi_sin, -1.0)
 

time: 1800 us -> 1680 us (0.933)
  local copies, waits for them, and re-layouts: 661 us -> 565 us
  other arithmetic: 125 us -> 97 us
    unnamed x30 -> x41, local copies, waits for them, and re-layouts: 181 us -> 106 us
    all_to_all x2 -> x0, local copies, waits for them, and re-layouts: 40.5 us -> none  [shards(): lax.all_to_all(imag_part, 'pz', split_axis=2, concat_axis=1, tiled=True)]
    all_to_all x1 -> x0, other arithmetic: 28.2 us -> none  [shards(): lax.all_to_all(imag_part, 'pz', split_axis=2, concat_axis=1, tiled=True)]
    transpose x0 -> x1, local copies, waits for them, and re-layouts: none -> 19.6 us  [relay_back(): values.reshape(batch, ky_block, x_block, pz_count, z_local)]
    all_to_all x1 -> x2, local copies, waits for them, and re-layouts: 40 us -> 40.5 us  [shards(): lax.all_to_all(real_part, 'pz', split_axis=2, concat_axis=1, tiled=True)]
  transfers between devices with their start and end apart: 12 -> 12, of which waited for: 11 -> 11; matrix products, arithmetic and copies ran while one was open for 33% -> 35% of each run, Pallas kernels for 0% -> 0%
where the time goes in v1:
time: 1680 us; the launch traced here: 1670 us
  local copies, waits for them, and re-layouts  565 us (34%)
  waiting for transfers between devices  536 us (32%)
  matrix products  415 us (25%)
  other arithmetic  97 us (6%)
  starting transfers between devices  51 us (3%)
    dot_general x20, matrix products, contract(): return jnp.einsum(form, data, table, precision=HIGH)  357 us
    all_to_all x1, waiting for transfers between devices, shards(): lax.all_to_all(real_part, 'pz', split_axis=1, concat_axis=2, tiled=True)  151 us
    unnamed x41, local copies, waits for them, and re-layouts  106 us
    all_to_all x1, waiting for transfers between devices, shards(): lax.all_to_all(real_part, 'pz', split_axis=2, concat_axis=1, tiled=True)  88.9 us
    all_to_all x1, waiting for transfers between devices, shards(): lax.all_to_all(real_part, 'py', split_axis=2, concat_axis=1, tiled=True)  68 us
    all_to_all x1, waiting for transfers between devices, shards(): lax.all_to_all(imag_part, 'py', split_axis=1, concat_axis=2, tiled=True)  62.9 us
    all_to_all x1, waiting for transfers between devices, shards(): lax.all_to_all(jnp.stack(jnp.split(imag_part, lax.axis_size('pz'), axis=2...  60.3 us
    dot_general x1, matrix products, make_kernel(): kernel = jnp.einsum('abr,rkxm->abkxm', coef, basis, precision=HIGH)  58.6 us
  transfers between devices with their start and end apart: 12, of which 11 were waited for; matrix products, arithmetic and copies ran while one was open for 35% of the time, Pallas kernels for 0%

profile of v1, /device:TPU:0, one launch (start us, length us, event | category | flops | bytes accessed | tf_op | source)
XLA Modules:
  0.0 1666.0 jit_solution(7886279953638968034)
XLA Ops:
  56.7 36.3 %convolution_bitcast_fusion = f32[2,512,2048]{2,1,0:T(8,128)S(1)} fusion(f32[2,2048,512]{2,1,0:T(8,128)} %bitcast.250, s32[512]{0:T(512)S(1)} %fusion.146), kind=kOutput, calls=%fused_computation.64 | convolution fusion | flops 12888571904 | bytes 16779264 | tf_op jit(solution)/shard_map/bsx,xq->bqs/dot_general | solution.py:48
  109.8 48.6 %multiply_bitcast_fusion = f32[2,512,2048]{2,1,0:T(8,128)S(1)} fusion(f32[2,2048,512]{2,1,0:T(8,128)} %bitcast.251, s32[512]{0:T(512)S(1)} %fusion.146), kind=kOutput, calls=%fused_computation.54 | convolution fusion | flops 12890669056 | bytes 16779264 | tf_op jit(solution)/shard_map/bsx,xq->bqs/dot_general | solution.py:48
  169.6 33.0 %all-to-all-done = f32[2,512,2048]{2,0,1:T(2,128)} async-done(((f32[2,512,2048]{2,0,1:T(2,128)}), f32[2,512,2048]{2,0,1:T(2,128)}, u32[]{:S(2)}, u32[]{:S(2)}) %all-to-all-start) | async-done | bytes 8388640 | tf_op jit(solution)/shard_map/all_to_all | solution.py:94
  238.9 62.9 %all-to-all-done.1 = f32[2,512,2048]{2,0,1:T(2,128)} async-done(((f32[2,512,2048]{2,0,1:T(2,128)}), f32[2,512,2048]{2,0,1:T(2,128)}, u32[]{:S(2)}, u32[]{:S(2)}) %all-to-all-start.1) | async-done | bytes 8388640 | tf_op jit(solution)/shard_map/all_to_all | solution.py:95
  406.3 150.7 %all-to-all-done.2 = f32[2,256,4096]{2,0,1:T(2,128)} async-done(((f32[2,256,4096]{2,0,1:T(2,128)}), f32[2,256,4096]{2,0,1:T(2,128)}, u32[]{:S(2)}, u32[]{:S(2)}) %all-to-all-start.2) | async-done | bytes 8388640 | tf_op jit(solution)/shard_map/all_to_all | solution.py:105
  563.9 58.6 %fusion.10 = f32[2,2,32,128,256]{4,1,0,3,2:T(2,128)} fusion(f32[8]{0:T(128)S(1)} %add_multiply_fusion, f32[32,128,256]{2,1,0:T(8,128)S(1)} %sqrt_multiply_fusion, f32[2,2,8]{2,1,0:T(2,128)S(1)} %copy-done), kind=kOutput, calls=%fused_computation.19 | convolution fusion | flops 436207616 | bytes 20971680 | tf_op jit(solution)/shard_map/abr,rkxm->abkxm/dot_general | solution.py:67
  622.6 20.3 %fusion.254 = (f32[2,1,32,128,256]{4,1,0,3,2:T(1,128)}, f32[2,1,32,128,256]{4,1,0,3,2:T(1,128)}) fusion(f32[2,2,32,128,256]{4,1,0,3,2:T(2,128)} %fusion.10), kind=kLoop, calls=%fused_computation.318 | loop fusion | bytes 33554432 | tf_op jit(solution)/shard_map/slice | solution.py:128
  654.4 20.1 %reshape.297 = f32[2,32,8,128,32]{4,3,2,1,0:T(8,128)} reshape(f32[2,32,8,4096]{3,2,1,0:T(8,128)} %bitcast.259) | data formatting | bytes 16777216 | tf_op jit(solution)/shard_map/reshape | solution.py:110
  674.5 21.7 %copy.138 = f32[2,32,128,8,32]{2,4,3,1,0:T(8,128)} copy(f32[2,32,128,8,32]{4,2,3,1,0:T(8,128)} %bitcast.230) | data formatting | bytes 16777216 | tf_op jit(solution)/shard_map/transpose | solution.py:110
  716.0 30.2 %all-to-all-done.3 = f32[2,256,4096]{2,0,1:T(2,128)} async-done(((f32[2,256,4096]{2,0,1:T(2,128)}), f32[2,256,4096]{2,0,1:T(2,128)}, u32[]{:S(2)}, u32[]{:S(2)}) %all-to-all-start.3) | async-done | bytes 8388640 | tf_op jit(solution)/shard_map/all_to_all | solution.py:106
  777.8 21.7 %copy.145 = f32[2,32,128,8,32]{2,4,3,1,0:T(8,128)} copy(f32[2,32,128,8,32]{4,2,3,1,0:T(8,128)} %bitcast.231) | data formatting | bytes 16777216 | tf_op jit(solution)/shard_map/transpose | solution.py:110
  819.0 21.1 %convolution_add_fusion = f32[2,32,128,256]{3,2,1,0:T(8,128)} fusion(f32[2,32,128,256]{3,2,1,0:T(8,128)} %fusion.98, f32[2,32,128,256]{2,3,1,0:T(8,128)S(1)} %bitcast.243, s32[256]{0:T(256)S(1)} %compare_select_fusion.8), kind=kOutput, calls=%fused_computation.71 | convolution fusion | flops 6445465600 | bytes 25166848 | tf_op jit(solution)/shard_map/bkxz,zm->bkxm/dot_general | solution.py:48
  866.0 30.3 %fusion.27 = (f32[2,32,128,256]{3,0,2,1:T(2,128)}, f32[2,32,128,256]{3,0,2,1:T(2,128)}) fusion(f32[2,1,32,128,256]{4,1,0,3,2:T(1,128)} %get-tuple-element.5, f32[2,1,32,128,256]{4,1,0,3,2:T(1,128)} %get-tuple-element.4, f32[32,128,256]{2,1,0:T(8,128)} %get-tuple-element.20, f32[32,128,256]{2,1,0:T(8,128)} %get-tuple-element.21, ...), kind=kLoop, calls=%fused_computation.44 | loop fusion | flops 12582912 | bytes 50331648 | tf_op jit(solution)/shard_map/add | solution.py:128
  929.5 28.7 %copy.206 = f32[2,32,8,128,32]{1,0,4,3,2:T(2,128)} copy(f32[2,32,8,128,32]{3,4,2,1,0:T(8,128)} %bitcast.261) | data formatting | bytes 16777216 | tf_op jit(solution)/shard_map/reshape | solution.py:140
  958.2 35.4 %reshape.329 = f32[8,1,262144]{2,1,0:T(1,128)} reshape(f32[32768,2,32]{2,1,0:T(2,128)} %bitcast.232) | data formatting | bytes 16777216
  1054.2 21.2 %reshape.304 = f32[2,32,32768]{2,1,0:T(8,128)} reshape(f32[2,32,8,128,32]{4,3,2,1,0:T(8,128)} %copy.166) | data formatting | bytes 16777216 | tf_op jit(solution)/shard_map/reshape | solution.py:140
  1093.7 88.9 %all-to-all-done.4 = f32[8,1,262144]{2,1,0:T(1,128)} async-done(((f32[8,1,262144]{2,1,0:T(1,128)}), f32[8,1,262144]{2,1,0:T(1,128)}, u32[]{:S(2)}, u32[]{:S(2)}) %all-to-all-start.4) | async-done | bytes 8388640 | tf_op jit(solution)/shard_map/all_to_all | solution.py:144
  1188.1 28.2 %reduce = f32[8,262144]{1,0:T(8,128)} reduce(f32[8,1,262144]{2,1,0:T(1,128)} %all-to-all-done.4, f32[]{:T(128)} %broadcast.767), dimensions={1}, to_apply=%all_to_all.98.reduce_sub_computation | reduce | bytes 16777220 | tf_op jit(solution)/shard_map/all_to_all | solution.py:144
  1216.3 54.9 %reshape.330 = f32[32768,2,32]{2,1,0:T(2,128)} reshape(f32[8,262144]{1,0:T(8,128)} %reduce) | data formatting | bytes 16777216
  1271.1 40.0 %copy.208 = f32[2,32,8,4096]{3,1,2,0:T(8,128)} copy(f32[2,32,8,4096]{1,0,3,2:T(2,128)} %bitcast.233) | data formatting | bytes 16777216 | tf_op jit(solution)/shard_map/all_to_all | solution.py:144
  1311.1 60.3 %all-to-all-done.5 = f32[8,2,32,4096]{3,2,1,0:T(8,128)} async-done(((f32[8,2,32,4096]{3,2,1,0:T(8,128)}), f32[8,2,32,4096]{3,2,1,0:T(8,128)}, u32[]{:S(2)}, u32[]{:S(2)}) %all-to-all-start.5) | async-done | bytes 8388640 | tf_op jit(solution)/shard_map/all_to_all | solution.py:146
  1504.3 30.8 %all-to-all-done.7 = f32[2,128,8192]{1,0,2:T(2,128)} async-done(((f32[2,128,8192]{1,0,2:T(2,128)}), f32[2,128,8192]{1,0,2:T(2,128)}, u32[]{:S(2)}, u32[]{:S(2)}) %all-to-all-start.7) | async-done | bytes 8388640 | tf_op jit(solution)/shard_map/all_to_all | solution.py:159
  1564.6 68.0 %all-to-all-done.6 = f32[2,128,8192]{1,0,2:T(2,128)} async-done(((f32[2,128,8192]{1,0,2:T(2,128)}), f32[2,128,8192]{1,0,2:T(2,128)}, u32[]{:S(2)}, u32[]{:S(2)}) %all-to-all-start.6) | async-done | bytes 8388640 | tf_op jit(solution)/shard_map/all_to_all | solution.py:158
  1640.3 21.1 %fusion.37 = f32[2,2048,512]{2,1,0:T(8,128)S(1)} fusion(f32[2,2048,512]{2,1,0:T(8,128)S(1)} %copy-done.8, f32[2,4,256,8,128]{4,3,2,1,0:T(8,128)} %bitcast.258, s32[512]{0:T(512)S(1)} %copy-done.11), kind=kOutput, calls=%fused_computation.69 | convolution fusion | flops 12890931200 | bytes 25167872 | tf_op jit(solution)/shard_map/bqs,qx->bsx/dot_general | solution.py:48
  (118 shorter events, 631.6 us)
Async XLA Ops:
  0.6 563.3 %copy-start = (f32[2,2,8]{2,1,0:T(2,128)S(1)}, f32[2,2,8]{2,1,0:T(2,128)}, u32[]{:S(2)}) copy-start(f32[2,2,8]{2,1,0:T(2,128)} %param.5) | copy-start | bytes 388
  0.6 13.5 copy-start.6
  0.7 13.5 copy-start.7
  25.8 8.3 collective-permute-start
  28.8 7.5 collective-permute-start.1
  36.9 8.5 collective-permute-start.2
  36.9 8.5 collective-permute-start.3
  40.5 69.3 %copy-start.10 = (s32[512]{0:T(512)}, s32[512]{0:T(512)S(1)}, u32[]{:S(2)}) copy-start(s32[512]{0:T(512)S(1)} %fusion.146) | copy-start | bytes 6148
  104.1 98.5 %all-to-all-start = ((f32[2,512,2048]{2,0,1:T(2,128)}), f32[2,512,2048]{2,0,1:T(2,128)}, u32[]{:S(2)}, u32[]{:S(2)}) async-start(f32[2,512,2048]{2,0,1:T(2,128)} %copy.125), calls=%async_computation | async-start | bytes 16777216 | tf_op jit(solution)/shard_map/all_to_all | solution.py:94
  202.6 99.2 %all-to-all-start.1 = ((f32[2,512,2048]{2,0,1:T(2,128)}), f32[2,512,2048]{2,0,1:T(2,128)}, u32[]{:S(2)}, u32[]{:S(2)}) async-start(f32[2,512,2048]{2,0,1:T(2,128)} %copy.131), calls=%async_computation.1 | async-start | bytes 16777216 | tf_op jit(solution)/shard_map/all_to_all | solution.py:95
  332.5 13.9 copy-start.4
  367.9 189.0 %all-to-all-start.2 = ((f32[2,256,4096]{2,0,1:T(2,128)}), f32[2,256,4096]{2,0,1:T(2,128)}, u32[]{:S(2)}, u32[]{:S(2)}) async-start(f32[2,256,4096]{2,0,1:T(2,128)} %copy.136), calls=%async_computation.2 | async-start | bytes 16777216 | tf_op jit(solution)/shard_map/all_to_all | solution.py:105
  557.0 189.2 %all-to-all-start.3 = ((f32[2,256,4096]{2,0,1:T(2,128)}), f32[2,256,4096]{2,0,1:T(2,128)}, u32[]{:S(2)}, u32[]{:S(2)}) async-start(f32[2,256,4096]{2,0,1:T(2,128)} %copy.143), calls=%async_computation.3 | async-start | bytes 16777216 | tf_op jit(solution)/shard_map/all_to_all | solution.py:106
  799.5 19.5 %copy-start.2 = (f32[2,32,128,8,32]{2,4,3,1,0:T(8,128)S(1)}, f32[2,32,128,8,32]{2,4,3,1,0:T(8,128)}, u32[]{:S(2)}) copy-start(f32[2,32,128,8,32]{2,4,3,1,0:T(8,128)} %copy.145) | copy-start | bytes 25165828
  799.5 40.6 %slice-start.2 = ((s8[8388608]{0:T(1024)(128)(4,1)}), s8[4194304]{0:T(1024)(128)(4,1)S(1)}, s32[]{:S(2)}) async-start(s8[8388608]{0:T(1024)(128)(4,1)} %bitcast.239), calls=%async_computation.10 | async-start | bytes 8388608
  819.0 21.1 %slice-start.3 = ((s8[8388608]{0:T(1024)(128)(4,1)}), s8[4194304]{0:T(1024)(128)(4,1)S(1)}, s32[]{:S(2)}) async-start(s8[8388608]{0:T(1024)(128)(4,1)} %bitcast.239), calls=%async_computation.11 | async-start | bytes 8388608
  840.1 18.4 %copy-start.9 = (f32[2,32,128,256]{3,2,1,0:T(8,128)S(1)}, f32[2,32,128,256]{3,2,1,0:T(8,128)}, u32[]{:S(2)}) copy-start(f32[2,32,128,256]{3,2,1,0:T(8,128)} %convolution_add_fusion) | copy-start | bytes 25165828
  896.2 13.0 copy-start.5
  993.6 189.0 %all-to-all-start.4 = ((f32[8,1,262144]{2,1,0:T(1,128)}), f32[8,1,262144]{2,1,0:T(1,128)}, u32[]{:S(2)}, u32[]{:S(2)}) async-start(f32[8,1,262144]{2,1,0:T(1,128)} %reshape.329), calls=%async_computation.4 | async-start | bytes 16777216 | tf_op jit(solution)/shard_map/all_to_all | solution.py:144
  1182.6 188.8 %all-to-all-start.5 = ((f32[8,2,32,4096]{3,2,1,0:T(8,128)}), f32[8,2,32,4096]{3,2,1,0:T(8,128)}, u32[]{:S(2)}, u32[]{:S(2)}) async-start(f32[8,2,32,4096]{3,2,1,0:T(8,128)} %fusion.52), calls=%async_computation.5 | async-start | bytes 16777216 | tf_op jit(solution)/shard_map/all_to_all | solution.py:146
  1371.4 15.6 slice-start
  1436.9 98.1 %all-to-all-start.7 = ((f32[2,128,8192]{1,0,2:T(2,128)}), f32[2,128,8192]{1,0,2:T(2,128)}, u32[]{:S(2)}, u32[]{:S(2)}) async-start(f32[2,128,8192]{1,0,2:T(2,128)} %copy.175), calls=%async_computation.7 | async-start | bytes 16777216 | tf_op jit(solution)/shard_map/all_to_all | solution.py:159
  1535.0 97.6 %all-to-all-start.6 = ((f32[2,128,8192]{1,0,2:T(2,128)}), f32[2,128,8192]{1,0,2:T(2,128)}, u32[]{:S(2)}, u32[]{:S(2)}) async-start(f32[2,128,8192]{1,0,2:T(2,128)} %copy.170), calls=%async_computation.6 | async-start | bytes 16777216 | tf_op jit(solution)/shard_map/all_to_all | solution.py:158
  1640.3 25.5 %copy-start.1 = (f32[2,2,8]{2,1,0:T(2,128)S(1)}, f32[2,2,8]{2,1,0:T(2,128)}, u32[]{:S(2)}) copy-start(f32[2,2,8]{2,1,0:T(2,128)} %param.5) | copy-start | bytes 388
  (4 other events, 34.6 us)
